TPU v7x, 256 devices: a whole 4x4x8 slice. The times are simulated.
256 devices in a mesh: col: 16 (over z, core), row: 16 (over x, y).
Axes of the slice: x: 4, y: 4, z: 8, core: 2. Of those that a mesh axis runs over, the one named last changes fastest.
Arguments:
- lower_cols: float32 [4096, 2048], P('col', 'row'), may hold values from -6 to 6
- pivot_rows: float32 [8192, 4096], P('row', 'col')
- pattern: int32 [64, 32], replicated, may hold values 0 or 1
- panel_in: float32 [8192, 2048], P('col', 'row'), may hold values from -6 to 6
- diag_in: float32 [64, 128, 128], P('col'), as said below
Outputs:
- panel: float32 [8192, 2048], P('col', 'row')
- factor: float32 [64, 128, 128], P('col')
Inputs may be any that keep to these rules, and one draw needn't show every extreme that they name: diag_in holds symmetric blocks with diagonal entries between 2.5 and 4.5; diag_in[j] - dsum[j] is positive definite.
All inputs are finite; a program needn't handle non-finite values.
Results may differ from a plain program's by a relative error of at most 0.00005.
Values sent between devices are 32-bit elements; how exact they have to be, the bound alone decides.
A program may use at most 128 MiB of HBM per device.

v0:
```python
import jax
import jax.numpy as jnp
from jax import lax
from jax.sharding import PartitionSpec as P

B = 128


def shards(lower_cols, pivot_rows, pattern, panel_in, diag_in):
    col_index = lax.axis_index("col")
    k_local = lower_cols.shape[0] // B
    targets = pattern.shape[0]
    own_targets = diag_in.shape[0]
    width = panel_in.shape[1]
    whole_pivot = lax.all_gather(pivot_rows, "row", axis=0, tiled=True)
    local_pattern = lax.dynamic_slice_in_dim(pattern, col_index * k_local, k_local, 1).astype(
        jnp.float32
    )
    masked = whole_pivot.reshape(targets, B, k_local, B) * local_pattern[:, None, :, None]
    masked = masked.reshape(targets * B, k_local * B)
    update = lax.psum_scatter(
        jnp.dot(
            masked, lower_cols, precision=lax.Precision.HIGHEST, preferred_element_type=jnp.float32
        ),
        "col",
        scatter_dimension=0,
        tiled=True,
    )
    blocks = masked.reshape(targets, B, k_local * B)
    partial_diag = jnp.einsum("jak,jbk->jab", blocks, blocks, precision=lax.Precision.HIGHEST)
    dsum = lax.psum_scatter(partial_diag, "col", scatter_dimension=0, tiled=True)
    factor = jnp.linalg.cholesky(diag_in - dsum)
    residue = (panel_in - update).reshape(own_targets, B, width)
    solved = lax.linalg.triangular_solve(factor, residue, left_side=True, lower=True)
    return (solved.reshape(own_targets * B, width), factor)


def solution(mesh):
    in_specs = (P("col", "row"), P("row", "col"), P(), P("col", "row"), P("col", None, None))
    out_specs = (P("col", "row"), P("col", None, None))
    return jax.shard_map(shards, mesh=mesh, in_specs=in_specs, out_specs=out_specs, check_vma=False)
```

profile of v0, /device:TPU:22, one launch (start us, length us, event | category | flops | bytes accessed | tf_op | source)
XLA Modules:
  0.0 266.2 jit_solution(10246708308004626296)
XLA Ops:
  7.2 0.0 all-gather.2.cloned.1.call-start
  7.2 0.7 all-gather.2.cloned.1.call-update
  7.9 0.0 reduce-scatter.3.cloned.1.call-start
  8.0 0.7 dynamic-slice_convert_fusion
  8.7 0.1 copy.13
  8.8 0.1 mul.24
  8.9 78.5 %all-gather.2.cloned.1.call-done = f32[8192,256]{1,0:T(8,128)} async-done(((f32[512,256]{1,0:T(8,128)}), f32[8192,256]{1,0:T(8,128)}) %all-gather.2.cloned.1.call-update) | async-done | bytes 8388624 | tf_op jit(solution)/shard_map/all_gather | solution.py:15
  87.4 16.6 %fusion.2 = f32[64,128,128]{1,2,0:T(8,128)} fusion(f32[64,128,256]{2,1,0:T(8,128)} %bitcast.23, f32[64,256]{1,0:T(8,128)S(1)} %bitcast.26), kind=kOutput, calls=%fused_computation.3 | convolution fusion | flops 3223322624 | bytes 12648448 | tf_op jit(solution)/shard_map/jak,jbk->jab/dot_general | solution.py:30
  104.0 0.0 reduce-scatter.3.cloned.1.call-update
  104.1 0.0 reduce-scatter.5.cloned.1.call-start
  104.1 5.4 %mul.28 = f32[64,128,2,128]{3,2,1,0:T(2,128)} broadcast(f32[64,2]{1,0:T(8,128)S(1)} %copy.13), dimensions={0,2} | broadcast | bytes 8389120 | tf_op jit(solution)/shard_map/mul | solution.py:19
  109.6 12.2 %fusion = f32[8192,128]{1,0:T(8,128)} fusion(f32[256,128]{1,0:T(8,128)S(1)} %copy-done, f32[8192,256]{1,0:T(8,128)} %all-gather.2.cloned.1.call-done, f32[1024,8,2,128]{3,2,1,0:T(2,128)} %bitcast.24), kind=kOutput, calls=%fused_computation.1 | convolution fusion | flops 3223322624 | bytes 21102592 | tf_op jit(solution)/shard_map/dot_general | solution.py:22
  121.8 0.0 reduce-scatter.5.cloned.1.call-update
  121.8 0.1 copy.15
  122.0 47.0 %reduce-scatter.3.cloned.1.call-done = f32[4,128,128]{1,2,0:T(8,128)} async-done(((f32[64,128,128]{1,2,0:T(8,128)}), f32[4,128,128]{1,2,0:T(8,128)}) %reduce-scatter.3.cloned.1.call-update) | async-done | bytes 262160 | tf_op jit(solution)/shard_map/reduce_scatter | solution.py:31
  169.0 1.0 sub.6
  169.9 0.1 copy.16
  170.1 46.9 %custom-call.7 = f32[4,128,128]{2,1,0:T(8,128)S(1)} custom-call(f32[4,128,128]{2,1,0:T(8,128)S(1)} %fusion.7), custom_call_target="Cholesky" | custom-call | tf_op jit(solution)/shard_map/jit(cholesky)/cholesky | solution.py:32
  217.1 0.1 compare_reduce_fusion
  217.2 0.8 select_bitcast_fusion
  218.0 39.3 %custom-call.8 = f32[4,1,128,128]{2,3,1,0:T(8,128)S(1)} custom-call(f32[4,1,128,128]{3,2,1,0:T(8,128)S(1)} %get-tuple-element.2), custom_call_target="InvertDiagBlocksLowerTriangular" | custom-call | tf_op jit(solution)/shard_map/triangular_solve | solution.py:34
  257.3 0.0 reduce-scatter.5.cloned.1.call-done
  257.3 1.0 sub.7
  258.3 1.3 fusion.5
  (11 shorter events, 0.1 us)
Async XLA Ops:
  7.2 102.4 %copy-start = (f32[256,128]{1,0:T(8,128)S(1)}, f32[256,128]{1,0:T(8,128)}, u32[]{:S(2)}) copy-start(f32[256,128]{1,0:T(8,128)} %param.5) | copy-start | bytes 393220
  7.2 80.3 %all-gather.2.cloned.1.call-start = ((), (), s32[]{:S(2)}) async-start(), calls=%async_computation.2 | async-start | bytes 8912896 | tf_op jit(solution)/shard_map/all_gather | solution.py:15
  7.9 161.1 %reduce-scatter.3.cloned.1.call-start = ((), (), s32[]{:S(2)}) async-start(), calls=%async_computation.3 | async-start | bytes 4456448 | tf_op jit(solution)/shard_map/reduce_scatter | solution.py:31
  104.1 153.3 %reduce-scatter.5.cloned.1.call-start = ((), (), s32[]{:S(2)}) async-start(), calls=%async_computation.4 | async-start | bytes 4456448 | tf_op jit(solution)/shard_map/reduce_scatter | solution.py:21
  109.6 12.2 %copy-start.2 = (f32[4,128,128]{2,1,0:T(8,128)S(1)}, f32[4,128,128]{2,1,0:T(8,128)}, u32[]{:S(2)}) copy-start(f32[4,128,128]{2,1,0:T(8,128)} %param.9) | copy-start | bytes 786436
  109.6 147.8 %copy-start.1 = (f32[512,128]{1,0:T(8,128)S(1)}, f32[512,128]{1,0:T(8,128)}, u32[]{:S(2)}) copy-start(f32[512,128]{1,0:T(8,128)} %param.8) | copy-start | bytes 786436
Sparse Core Ops, SparseCore 0:
  10.4 76.9 all-gather.1
  104.2 64.7 reduce-scatter.2
  171.5 62.2 reduce-scatter.4
where the time goes:
time: 267 us; the launch traced here: 266 us
  waiting for transfers between devices  126 us (47%)
  other arithmetic  89.9 us (34%)
  matrix products  30.1 us (11%)
  between operations  13.8 us (5%)
  local copies, waits for them, and re-layouts  5.94 us (2%)
    all_gather x1, waiting for transfers between devices, shards(): whole_pivot = lax.all_gather(pivot_rows, 'row', axis=0, tiled=True)  78.5 us
    another operation x4, other arithmetic, shards(): factor = jnp.linalg.cholesky(diag_in - dsum)  47.1 us
    reduce_scatter x1, waiting for transfers between devices, shards(): lax.psum_scatter(partial_diag, 'col', scatter_dimension=0, tiled=True)  47 us
    another operation x3, other arithmetic, shards(): lax.linalg.triangular_solve(factor, residue, left_side=True, lower=True)  40.1 us
    dot_general x1, matrix products, shards(): jnp.einsum('jak,jbk->jab', blocks, blocks, precision=lax.Precision.HIGHEST)  16.6 us
    dot_general x1, matrix products, shards(): jnp.dot(masked, lower_cols, precision=lax.Precision.HIGHEST, preferred_el...  12.2 us
    mul x2, local copies, waits for them, and re-layouts, shards(): whole_pivot.reshape(targets, B, k_local, B)  5.56 us
  transfers between devices with their start and end apart: 3, of which 2 were waited for; matrix products, arithmetic and copies ran while one was open for 40% of the time, Pallas kernels for 0%

commit v1 on v0

v1 whole, which is shorter than its diff:
```python
import jax
import jax.numpy as jnp
from jax import lax
from jax.experimental import pallas as pl
from jax.experimental.pallas import tpu as pltpu
from jax.sharding import PartitionSpec as P

B = 128
NR = 4
RB = 64
F32 = jnp.float32
BF16 = jnp.bfloat16
MESH = pl.DeviceIdType.MESH
HIGHEST = lax.Precision.HIGHEST


def split(v):
    hi = v.astype(BF16)
    return hi, (v - hi.astype(F32)).astype(BF16)


def move_kernel(
    pat, piv, low, pan, dia, res_o, sm_o,
    ag, bg, bh, bl, lh, ll, part, sd, su, upd, ds, dsd, dsu, sb,
    a_ss, a_rs, af_ss, b_ss, b_rs, r_ss, rd_rs, ru_rs, d_ss, dd_rs, du_rs,
    s1_ss, s1_rs, s2_ss, s2_rs, y_ss, y_rs,
):
    c_me = lax.axis_index("col")
    r_me = lax.axis_index("row")
    z, h = c_me // 2, c_me % 2
    x, y = r_me // 4, r_me % 4
    oh = 1 - h
    xp, xm, xo = (x + 1) % 4, (x + 3) % 4, (x + 2) % 4
    yp, ym, yo = (y + 1) % 4, (y + 3) % 4, (y + 2) % 4
    zp, zm = (z + 1) % 8, (z + 7) % 8
    yh = y // 2

    def dev(zz, hh, xx, yy):
        return (2 * zz + hh, 4 * xx + yy)

    def rcopy(src, dst, ss, rs, to):
        return pltpu.make_async_remote_copy(
            src_ref=src, dst_ref=dst, send_sem=ss, recv_sem=rs, device_id=to, device_id_type=MESH
        )

    here = dev(z, oh, x, y)

    def arrived(slot, ss, rs):
        rcopy(slot, slot, ss, rs, here).wait_recv()

    peers = [here, dev(zp, h, x, y), dev(zm, h, x, y)]
    for hh in (h, oh):
        peers += [dev(z, hh, xx, y) for xx in (xp, xm, xo)]
        peers += [dev(z, hh, x, yy) for yy in (yp, ym, yo)]
    bar = pltpu.get_barrier_semaphore()
    for p in peers:
        pl.semaphore_signal(bar, inc=1, device_id=p, device_id_type=MESH)
    pl.semaphore_wait(bar, len(peers))

    def rows(hh, i):
        return pl.ds(pl.multiple_of(2 * B * hh + RB * i, RB), RB)

    pending = []

    def go(c):
        c.start()
        pending.append(c)

    for i in range(NR):
        go(rcopy(piv.at[rows(oh, i)], ag.at[i, x, h], a_ss.at[i, 0], a_rs.at[i, 0, h], here))
    go(rcopy(low, bg.at[y, h], b_ss.at[0], b_rs.at[0], here))
    go(rcopy(low, bg.at[y, h], b_ss.at[1], b_rs.at[1], dev(z, h, x, yp)))
    go(rcopy(low, bg.at[y, h], b_ss.at[2], b_rs.at[2], dev(z, h, x, ym)))
    for i in range(NR):
        for n, hh in enumerate((h, oh)):
            src = piv.at[rows(hh, i)]
            go(rcopy(src, ag.at[i, x, h], a_ss.at[i, 1 + 2 * n], a_rs.at[i, 1, h], dev(z, hh, xp, y)))
            go(rcopy(src, ag.at[i, x, h], a_ss.at[i, 2 + 2 * n], a_rs.at[i, 2, h], dev(z, hh, xm, y)))
    for i in range(NR):
        ag[i, x, h] = piv[rows(h, i), :]
    bg[y, h] = low[...]

    def weight(xr, i, kap, kb):
        return pat[4 * (4 * xr + y) + 2 * h + i // 2, 2 * (2 * z + kap) + kb].astype(F32)

    for i in range(NR):
        arrived(ag.at[i, x, oh], a_ss.at[i, 0], a_rs.at[i, 0, oh])
    for t in range(2):
        m = jnp.concatenate(
            [
                jnp.concatenate(
                    [
                        ag[i, x, kap, :, kb * B : (kb + 1) * B] * weight(x, i, kap, kb)
                        for kap in range(2)
                        for kb in range(2)
                    ],
                    axis=1,
                )
                for i in (2 * t, 2 * t + 1)
            ],
            axis=0,
        )
        ds[t] = lax.dot_general(
            m, m, (((1,), (1,)), ((), ())), precision=HIGHEST, preferred_element_type=F32
        )

    d0 = (z - 2 * x - yh + 8) % 8

    def takes_down(d, s):
        return (d <= 3) if s == 0 else (d <= 2)

    def takes_up(d, s):
        return (d >= 6) | (d == 0) if s == 0 else (d >= 5) | (d == 0)

    def gives_down(d, s):
        return (d >= 1) & (d <= 4) if s == 0 else (d >= 1) & (d <= 3)

    def gives_up(d, s):
        return (d >= 5) if s == 0 else (d >= 4)

    def dsum_step(t, u):
        at = pl.ds(RB * u, RB)
        k = 2 * t + u

        @pl.when(takes_down(d0, t))
        def _():
            arrived(dsd.at[t, at], d_ss.at[k], dd_rs.at[k])
            ds[t, at, :] += dsd[t, at, :]

        @pl.when(takes_up(d0, t))
        def _():
            arrived(dsu.at[t, at], d_ss.at[k], du_rs.at[k])
            ds[t, at, :] += dsu[t, at, :]

        @pl.when(gives_down(d0, t))
        def _():
            rcopy(ds.at[t, at], dsd.at[t, at], d_ss.at[k], dd_rs.at[k], dev(zm, h, x, y)).start()

        @pl.when(gives_up(d0, t))
        def _():
            rcopy(ds.at[t, at], dsu.at[t, at], d_ss.at[k], du_rs.at[k], dev(zp, h, x, y)).start()

    def forward_b():
        arrived(bg.at[ym, h], b_ss.at[1], b_rs.at[1])
        go(rcopy(bg.at[ym, h, 0:B], bg.at[ym, h, 0:B], b_ss.at[3], b_rs.at[3], dev(z, h, x, yp)))
        go(rcopy(bg.at[ym, h], bg.at[ym, h], b_ss.at[5], b_rs.at[5], here))
        arrived(bg.at[yp, h], b_ss.at[2], b_rs.at[2])
        go(rcopy(bg.at[yp, h, B:], bg.at[yp, h, B:], b_ss.at[4], b_rs.at[4], dev(z, h, x, ym)))
        go(rcopy(bg.at[yp, h], bg.at[yp, h], b_ss.at[6], b_rs.at[6], here))

    def forward_b2():
        arrived(bg.at[yo, h, 0:B], b_ss.at[3], b_rs.at[3])
        go(rcopy(bg.at[yo, h, 0:B], bg.at[yo, h, 0:B], b_ss.at[7], b_rs.at[7], here))
        arrived(bg.at[yo, h, B:], b_ss.at[4], b_rs.at[4])
        go(rcopy(bg.at[yo, h, B:], bg.at[yo, h, B:], b_ss.at[8], b_rs.at[8], here))

    def build_b():
        arrived(bg.at[y, oh], b_ss.at[0], b_rs.at[0])
        arrived(bg.at[ym, oh], b_ss.at[5], b_rs.at[5])
        arrived(bg.at[yp, oh], b_ss.at[6], b_rs.at[6])
        arrived(bg.at[yo, oh, 0:B], b_ss.at[7], b_rs.at[7])
        arrived(bg.at[yo, oh, B:], b_ss.at[8], b_rs.at[8])
        for yy in range(4):
            for kap in range(2):
                hi, lo = split(bg[yy, kap])
                bh[kap * 256 : kap * 256 + 256, yy * B : yy * B + B] = hi
                bl[kap * 256 : kap * 256 + 256, yy * B : yy * B + B] = lo

    def forward_a(i):
        arrived(ag.at[i, xm, 0], a_ss.at[i, 0], a_rs.at[i, 1, 0])
        go(rcopy(ag.at[i, xm, 0], ag.at[i, xm, 0], af_ss.at[i, 0], a_rs.at[i, 3, 0], dev(z, h, xp, y)))
        arrived(ag.at[i, xp, 1], a_ss.at[i, 0], a_rs.at[i, 2, 1])
        go(rcopy(ag.at[i, xp, 1], ag.at[i, xp, 1], af_ss.at[i, 1], a_rs.at[i, 3, 1], dev(z, h, xm, y)))

    def product(i):
        arrived(ag.at[i, xm, 1], a_ss.at[i, 0], a_rs.at[i, 1, 1])
        arrived(ag.at[i, xp, 0], a_ss.at[i, 0], a_rs.at[i, 2, 0])
        arrived(ag.at[i, xo, 0], a_ss.at[i, 0], a_rs.at[i, 3, 0])
        arrived(ag.at[i, xo, 1], a_ss.at[i, 0], a_rs.at[i, 3, 1])
        for xr in range(4):
            for kap in range(2):
                for kb in range(2):
                    v = ag[i, xr, kap, :, kb * B : (kb + 1) * B] * weight(xr, i, kap, kb)
                    hi, lo = split(v)
                    k = (2 * kap + kb) * B
                    lh[xr * RB : xr * RB + RB, k : k + B] = hi
                    ll[xr * RB : xr * RB + RB, k : k + B] = lo
        p = jnp.dot(lh[...], bh[...], preferred_element_type=F32)
        p += jnp.dot(ll[...], bh[...], preferred_element_type=F32)
        p += jnp.dot(lh[...], bl[...], preferred_element_type=F32)
        for xr in range(4):
            part[i, xr] = p[xr * RB : xr * RB + RB]

    par = (z + yh) % 2
    e = (z - yh + 8) % 8
    offs = [jnp.where(par == 0, ev, od) for ev, od in ((4, 3), (2, 5), (6, 1), (0, 7))]
    blks = [((e - d + 8) // 2) % 4 for d in offs]

    def reduce_step(i, q, s, leaf):
        d, xr = offs[q], blks[q]
        at = pl.ds(256 * s, 256)
        mine = part.at[i, xr, :, at]
        ss = r_ss.at[i, q, s]
        tk_d, tk_u = takes_down(d, s), takes_up(d, s)
        if not leaf:

            @pl.when(tk_d)
            def _():
                arrived(sd.at[i, xr, s], ss, rd_rs.at[i, xr, s])
                part[i, xr, :, at] += sd[i, xr, s]

            @pl.when(tk_u)
            def _():
                arrived(su.at[i, xr, s], ss, ru_rs.at[i, xr, s])
                part[i, xr, :, at] += su[i, xr, s]

        first = jnp.logical_not(tk_d | tk_u)
        turn = first if leaf else jnp.logical_not(first)

        @pl.when(turn & gives_down(d, s))
        def _():
            rcopy(mine, sd.at[i, xr, s], ss, rd_rs.at[i, xr, s], dev(zm, h, x, y)).start()

        @pl.when(turn & gives_up(d, s))
        def _():
            rcopy(mine, su.at[i, xr, s], ss, ru_rs.at[i, xr, s], dev(zp, h, x, y)).start()

    c_to = y % 2
    owner = par == 0

    def leaves(i):
        for q in range(2):
            for s in range(2):
                reduce_step(i, q, s, True)

    def middle(i):
        @pl.when(par == 1)
        def _():
            reduce_step(i, 0, 0, False)
            reduce_step(i, 1, 1, False)

        @pl.when(par == 0)
        def _():
            reduce_step(i, 1, 1, False)
            reduce_step(i, 2, 0, False)
            reduce_step(i, 1, 0, False)
            reduce_step(i, 2, 1, False)

    def finish(i):
        @pl.when(par == 1)
        def _():
            for s in range(2):
                reduce_step(i, 2, s, False)
                reduce_step(i, 3, s, False)

        @pl.when(par == 0)
        def _():
            for s in range(2):
                reduce_step(i, 3, s, False)
                for yy in (2 * s, 2 * s + 1):
                    same = (yy == y) & (h == c_to)
                    src = part.at[i, blks[3], :, pl.ds(B * yy, B)]

                    @pl.when(same)
                    def _():
                        upd[rows(h, i), :] = part[i, blks[3], :, pl.ds(B * yy, B)]

                    @pl.when(jnp.logical_not(same))
                    def _():
                        rcopy(
                            src, upd.at[rows(h, i)], y_ss.at[i, yy], y_rs.at[i, h], dev(z, c_to, x, yy)
                        ).start()

    root = d0 == 0
    relay = owner & (h == c_to)

    def sum_x():
        @pl.when(root)
        def _():
            for t in range(2):
                for n, xx in enumerate((xp, xm, xo)):
                    rcopy(
                        ds.at[t], sb.at[2 * h + t], s1_ss.at[t, n], s1_rs.at[2 * h + t], dev(z, c_to, xx, y)
                    ).start()

                @pl.when(h != c_to)
                def _():
                    rcopy(ds.at[t], sb.at[2 * h + t], s1_ss.at[t, 3], s1_rs.at[2 * h + t], here).start()

                @pl.when(h == c_to)
                def _():
                    sb[2 * h + t] = ds[t]

    def sum_y():
        @pl.when(relay)
        def _():
            for t in range(4):
                @pl.when(jnp.logical_not(root & (h == t // 2)))
                def _():
                    arrived(sb.at[t], s1_ss.at[0, 0], s1_rs.at[t])

                for n, yy in enumerate((yp, ym, yo)):
                    rcopy(sb.at[t], sb.at[t], s2_ss.at[t, n], s2_rs.at[t], dev(z, h, x, yy)).start()

    forward_b()
    for t in range(2):
        for u in range(2):
            dsum_step(t, u)
    forward_a(0)
    forward_b2()
    sum_x()
    build_b()
    for i in range(NR):
        product(i)
        leaves(i)
        if i + 1 < NR:
            forward_a(i + 1)
        if i == 1:
            sum_y()
        if i > 0:
            finish(i - 1)
        middle(i)
    finish(NR - 1)

    @pl.when(jnp.logical_not(relay))
    def _():
        for t in range(4):
            arrived(sb.at[t], s2_ss.at[t, 0], s2_rs.at[t])

    sm_o[...] = dia[...] - sb[...]
    y_src = 2 * (z % 2) + h
    for i in range(NR):
        for hh in range(2):

            @pl.when(jnp.logical_not((y == y_src) & (h == hh)))
            def _():
                arrived(upd.at[rows(hh, i)], y_ss.at[i, 0], y_rs.at[i, hh])

            res_o[rows(hh, i), :] = pan[rows(hh, i), :] - upd[rows(hh, i), :]

    for c in pending:
        c.wait_send()
    for t in range(2):
        for u in range(2):
            k = 2 * t + u
            at = pl.ds(RB * u, RB)

            @pl.when(jnp.logical_not(root))
            def _():
                rcopy(ds.at[t, at], dsd.at[t, at], d_ss.at[k], dd_rs.at[k], here).wait_send()

    for i in range(NR):
        for q in range(4):
            for s in range(2):

                @pl.when(offs[q] != 0)
                def _():
                    rcopy(
                        part.at[i, blks[q], :, pl.ds(256 * s, 256)], sd.at[i, blks[q], s],
                        r_ss.at[i, q, s], rd_rs.at[i, blks[q], s], here,
                    ).wait_send()

        @pl.when(owner)
        def _():
            for yy in range(4):
                @pl.when(jnp.logical_not((yy == y) & (h == c_to)))
                def _():
                    rcopy(
                        part.at[i, blks[3], :, pl.ds(B * yy, B)], upd.at[rows(h, i)],
                        y_ss.at[i, yy], y_rs.at[i, h], here,
                    ).wait_send()

    @pl.when(root)
    def _():
        for t in range(2):
            for n in range(3):
                rcopy(ds.at[t], sb.at[t], s1_ss.at[t, n], s1_rs.at[t], here).wait_send()

            @pl.when(h != c_to)
            def _():
                rcopy(ds.at[t], sb.at[t], s1_ss.at[t, 3], s1_rs.at[t], here).wait_send()

    @pl.when(relay)
    def _():
        for t in range(4):
            for n in range(3):
                rcopy(sb.at[t], sb.at[t], s2_ss.at[t, n], s2_rs.at[t], here).wait_send()


def move(pattern, pivot_rows, lower_cols, panel_in, diag_in):
    vm = pl.BlockSpec(memory_space=pltpu.VMEM)
    dma = pltpu.SemaphoreType.DMA
    return pl.pallas_call(
        move_kernel,
        out_shape=(
            jax.ShapeDtypeStruct((4 * B, B), F32),
            jax.ShapeDtypeStruct((4, B, B), F32),
        ),
        in_specs=[pl.BlockSpec(memory_space=pltpu.SMEM)] + [vm] * 4,
        out_specs=(vm, vm),
        scratch_shapes=[
            pltpu.VMEM((NR, 4, 2, RB, 256), F32),
            pltpu.VMEM((4, 2, 256, B), F32),
            pltpu.VMEM((512, 512), BF16),
            pltpu.VMEM((512, 512), BF16),
            pltpu.VMEM((256, 512), BF16),
            pltpu.VMEM((256, 512), BF16),
            pltpu.VMEM((NR, 4, RB, 512), F32),
            pltpu.VMEM((NR, 4, 2, RB, 256), F32),
            pltpu.VMEM((NR, 4, 2, RB, 256), F32),
            pltpu.VMEM((4 * B, B), F32),
            pltpu.VMEM((2, B, B), F32),
            pltpu.VMEM((2, B, B), F32),
            pltpu.VMEM((2, B, B), F32),
            pltpu.VMEM((4, B, B), F32),
            dma((NR, 5)), dma((NR, 4, 2)), dma((NR, 2)), dma((9,)), dma((9,)),
            dma((NR, 4, 2)), dma((NR, 4, 2)), dma((NR, 4, 2)), dma((4,)), dma((4,)), dma((4,)),
            dma((2, 4)), dma((4,)), dma((4, 3)), dma((4,)), dma((NR, 4)), dma((NR, 2)),
        ],
        compiler_params=pltpu.CompilerParams(
            collective_id=0, has_side_effects=True, vmem_limit_bytes=48 << 20
        ),
        name="move",
    )(pattern, pivot_rows, lower_cols, panel_in, diag_in)


PB = 32


def factor_kernel(sm, res, out, fac, am, mi):
    row8 = lax.broadcasted_iota(jnp.int32, (8, B), 0)
    lane8 = lax.broadcasted_iota(jnp.int32, (8, B), 1)
    am[...] = sm[...]
    eye = (
        lax.broadcasted_iota(jnp.int32, (B, B), 0) == lax.broadcasted_iota(jnp.int32, (B, B), 1)
    ).astype(F32)
    for m in range(4):
        mi[m] = eye
    nv = PB // 8
    for b in range(B // PB):
        lo = PB * b
        ra = [[am[m, lo + 8 * v : lo + 8 * v + 8, :] for v in range(nv)] for m in range(4)]
        rm = [[mi[m, lo + 8 * v : lo + 8 * v + 8, :] for v in range(nv)] for m in range(4)]
        for i in range(PB):
            v0, s0 = i // 8, i % 8
            j = lo + i
            for m in range(4):
                row = ra[m][v0][s0 : s0 + 1, :]
                mrow = rm[m][v0][s0 : s0 + 1, :]
                cols = [
                    jnp.broadcast_to(ra[m][v][:, j : j + 1], (8, B)) if v >= v0 else None
                    for v in range(nv)
                ]
                inv = 1.0 / cols[v0][s0 : s0 + 1, :]
                row, mrow = row * inv, mrow * inv
                for v in range(v0, nv):
                    f = cols[v]
                    if v == v0:
                        if s0 == 7:
                            continue
                        f = jnp.where(row8 > s0, f, 0.0)
                    ra[m][v] = ra[m][v] - f * row
                    rm[m][v] = rm[m][v] - f * mrow
        for m in range(4):
            ls, ms = [], []
            for v in range(nv):
                on = lane8 - row8 - (lo + 8 * v)
                d = jnp.sum(jnp.where(on == 0, ra[m][v], 0.0), axis=1, keepdims=True)
                s = lax.rsqrt(d)
                s = s * (1.5 - 0.5 * d * s * s)
                ls.append(jnp.where(on >= 0, ra[m][v] * s, 0.0))
                ms.append(rm[m][v] * s)
            ls = jnp.concatenate(ls, axis=0)
            ms = jnp.concatenate(ms, axis=0)
            mi[m, lo : lo + PB, :] = ms
            lt = ls.T
            fac[m, :, lo : lo + PB] = lt
            if lo + PB < B:
                g = jnp.dot(
                    lt[lo + PB :, :],
                    jnp.concatenate([ls, ms], axis=1),
                    precision=HIGHEST,
                    preferred_element_type=F32,
                )
                am[m, lo + PB :, :] -= g[:, :B]
                mi[m, lo + PB :, :] -= g[:, B:]
    for m in range(4):
        out[m * B : m * B + B, :] = jnp.dot(
            mi[m], res[m * B : m * B + B, :], precision=HIGHEST, preferred_element_type=F32
        )


def factor_solve(sm, res):
    vm = pl.BlockSpec(memory_space=pltpu.VMEM)
    return pl.pallas_call(
        factor_kernel,
        out_shape=(
            jax.ShapeDtypeStruct((4 * B, B), F32),
            jax.ShapeDtypeStruct((4, B, B), F32),
        ),
        in_specs=[vm, vm],
        out_specs=(vm, vm),
        scratch_shapes=[pltpu.VMEM((4, B, B), F32), pltpu.VMEM((4, B, B), F32)],
        name="factor_solve",
    )(sm, res)


def shards(lower_cols, pivot_rows, pattern, panel_in, diag_in):
    res, sm = move(pattern, pivot_rows, lower_cols, panel_in, diag_in)
    return factor_solve(sm, res)


def solution(mesh):
    in_specs = (P("col", "row"), P("row", "col"), P(), P("col", "row"), P("col", None, None))
    out_specs = (P("col", "row"), P("col", None, None))
    return jax.shard_map(shards, mesh=mesh, in_specs=in_specs, out_specs=out_specs, check_vma=False)
```

time: 267 us -> 104 us (0.39)
  waiting for transfers between devices: 126 us -> 0 us
  Pallas kernels: 0 us -> 96.7 us
  other arithmetic: 89.9 us -> 0 us
  matrix products: 30.1 us -> 0 us
  between operations: 13.8 us -> 0.65 us
    pallas_call x0 -> x2, Pallas kernels: none -> 96.7 us  [the longest x1 82.5 us: move(): pl.pallas_call(move_kernel, out_shape=(jax.ShapeDtypeStruct((4 * B, B), F...]
    another operation x7 -> x0, other arithmetic: 87.2 us -> none  [the longest x4 47.1 us: shards(): factor = jnp.linalg.cholesky(diag_in - dsum)]
    all_gather x1 -> x0, waiting for transfers between devices: 78.5 us -> none  [shards(): whole_pivot = lax.all_gather(pivot_rows, 'row', axis=0, tiled=True)]
    reduce_scatter x2 -> x0, waiting for transfers between devices: 47 us -> none  [the longest x1 47 us: shards(): lax.psum_scatter(partial_diag, 'col', scatter_dimension=0, tiled=True)]
    dot_general x2 -> x0, matrix products: 28.8 us -> none  [the longest x1 16.6 us: shards(): jnp.einsum('jak,jbk->jab', blocks, blocks, precision=lax.Precision.HIGHEST)]
    unnamed x8 -> x13, local copies, waits for them, and re-layouts: 0.15 us -> 6.03 us
    mul x2 -> x0, local copies, waits for them, and re-layouts: 5.56 us -> none  [shards(): whole_pivot.reshape(targets, B, k_local, B)]
  transfers between devices with their start and end apart: 3 -> 0, of which waited for: 2 -> 0; matrix products, arithmetic and copies ran while one was open for 40% -> 0% of each run, Pallas kernels for 0% -> 0%
where the time goes in v1:
time: 104 us; the launch traced here: 103 us
  Pallas kernels  96.7 us (93%)
  local copies, waits for them, and re-layouts  6.03 us (6%)
    pallas_call x1, Pallas kernels, move(): pl.pallas_call(move_kernel, out_shape=(jax.ShapeDtypeStruct((4 * B, B), F...  82.5 us
    pallas_call x1, Pallas kernels, factor_solve(): pl.pallas_call(factor_kernel, out_shape=(jax.ShapeDtypeStruct((4 * B, B),...  14.2 us
    unnamed x13, local copies, waits for them, and re-layouts  6.03 us

profile of v1, /device:TPU:22, one launch (start us, length us, event | category | flops | bytes accessed | tf_op | source)
XLA Modules:
  0.0 103.4 jit_solution(12009355704502518024)
XLA Ops:
  0.6 0.8 copy.7.pat
  1.4 0.0 copy-start
  1.4 1.0 %copy-done = f32[512,256]{1,0:T(8,128)S(1)} copy-done((f32[512,256]{1,0:T(8,128)S(1)}, f32[512,256]{1,0:T(8,128)}, u32[]{:S(2)}) %copy-start) | copy-done | bytes 524312
  2.5 0.0 copy-start.1
  2.5 0.9 copy-done.1
  3.4 0.0 copy-start.2
  3.4 0.9 copy-done.2
  4.4 0.0 copy-start.5
  4.4 0.9 copy-done.5
  5.3 82.5 %move.1 = (f32[512,128]{1,0:T(8,128)S(1)}, f32[4,128,128]{2,1,0:T(8,128)S(1)}) custom-call(s32[64,32]{1,0:T(8,128)S(1)} %copy.7.pat, f32[512,256]{1,0:T(8,128)S(1)} %copy-done, f32[256,128]{1,0:T(8,128)S(1)} %copy-done.5, f32[512,128]{1,0:T(8,128)S(1)} %copy-done.1, f32[4,128,128]{2,1,0:T(8,128)S(1)} %copy-done.2), custom_call_target="tpu_custom_call" | custom-call | tf_op jit(solution)/shard_map/move/pallas_call | solution.py:393
  87.8 0.0 copy-start.3
  87.8 0.7 copy-done.3
  88.5 0.0 copy-start.4
  88.5 0.7 copy-done.4
  89.2 14.2 %factor_solve.1 = (f32[512,128]{1,0:T(8,128)}, f32[4,128,128]{2,1,0:T(8,128)}) custom-call(f32[4,128,128]{2,1,0:T(8,128)} %copy-done.4, f32[512,128]{1,0:T(8,128)} %copy-done.3), custom_call_target="tpu_custom_call" | custom-call | tf_op jit(solution)/shard_map/factor_solve/pallas_call | solution.py:495
Async XLA Ops:
  1.4 1.0 %copy-start = (f32[512,256]{1,0:T(8,128)S(1)}, f32[512,256]{1,0:T(8,128)}, u32[]{:S(2)}) copy-start(f32[512,256]{1,0:T(8,128)} %piv.1) | copy-start | bytes 1572868
  2.5 0.9 copy-start.1
  3.4 0.9 copy-start.2
  4.4 0.9 copy-start.5
  87.8 0.7 copy-start.3
  88.5 0.7 copy-start.4

commit v2 on v1

v2 whole, which is shorter than its diff:
```python
import jax
import jax.numpy as jnp
from jax import lax
from jax.experimental import pallas as pl
from jax.experimental.pallas import tpu as pltpu
from jax.sharding import PartitionSpec as P

B = 128
NR = 4
RB = 64
F32 = jnp.float32
BF16 = jnp.bfloat16
MESH = pl.DeviceIdType.MESH
HIGHEST = lax.Precision.HIGHEST


def split(v):
    hi = v.astype(BF16)
    return hi, (v - hi.astype(F32)).astype(BF16)


PB = 32


def factor_panel(b, am, mi, fac):
    row8 = lax.broadcasted_iota(jnp.int32, (8, B), 0)
    lane8 = lax.broadcasted_iota(jnp.int32, (8, B), 1)
    nv = PB // 8
    lo = PB * b
    ra = [[am[m, lo + 8 * v : lo + 8 * v + 8, :] for v in range(nv)] for m in range(4)]
    rm = [[mi[m, lo + 8 * v : lo + 8 * v + 8, :] for v in range(nv)] for m in range(4)]
    for v0 in range(nv):
        at = lo + 8 * v0
        cols = [
            [
                [jnp.broadcast_to(ra[m][v][:, at + k : at + k + 1], (8, B)) for v in range(v0, nv)]
                for k in range(8)
            ]
            for m in range(4)
        ]
        for k in range(8):
            for m in range(4):
                c = cols[m]
                inv = 1.0 / c[k][0][k : k + 1, :]
                row = ra[m][v0][k : k + 1, :] * inv
                mrow = rm[m][v0][k : k + 1, :] * inv
                scal = [c[kk][0][k : k + 1, :] * inv for kk in range(k + 1, 8)]
                for v in range(v0, nv):
                    f = c[k][v - v0]
                    if v == v0:
                        if k == 7:
                            continue
                        f = jnp.where(row8 > k, f, 0.0)
                    for kk in range(k + 1, 8):
                        c[kk][v - v0] = c[kk][v - v0] - f * scal[kk - k - 1]
                    ra[m][v] = ra[m][v] - f * row
                    rm[m][v] = rm[m][v] - f * mrow
    for m in range(4):
        ls, ms = [], []
        for v in range(nv):
            on = lane8 - row8 - (lo + 8 * v)
            d = jnp.sum(jnp.where(on == 0, ra[m][v], 0.0), axis=1, keepdims=True)
            s = lax.rsqrt(d)
            s = s * (1.5 - 0.5 * d * s * s)
            ls.append(jnp.where(on >= 0, ra[m][v] * s, 0.0))
            ms.append(rm[m][v] * s)
        ls = jnp.concatenate(ls, axis=0)
        ms = jnp.concatenate(ms, axis=0)
        mi[m, lo : lo + PB, :] = ms
        lt = ls.T
        fac[m, :, lo : lo + PB] = lt
        if lo + PB < B:
            g = jnp.dot(
                lt[lo + PB :, :],
                jnp.concatenate([ls, ms], axis=1),
                precision=HIGHEST,
                preferred_element_type=F32,
            )
            am[m, lo + PB :, :] -= g[:, :B]
            mi[m, lo + PB :, :] -= g[:, B:]


def window_kernel(
    pat_h, piv, low, pan_h, dia_h, out_h, fac_h,
    pat, ag, bg, bh, bl, lh, ll, part, sd, su, upd, ds, dsd, dsu, sb, pan, am, mi, fac, out,
    l_ss, a_ss, a_rs, af_ss, b_ss, b_rs, r_ss, rd_rs, ru_rs, d_ss, dd_rs, du_rs,
    s1_ss, s1_rs, s2_ss, s2_rs, y_ss, y_rs,
):
    c_me = lax.axis_index("col")
    r_me = lax.axis_index("row")
    z, h = c_me // 2, c_me % 2
    x, y = r_me // 4, r_me % 4
    oh = 1 - h
    xp, xm, xo = (x + 1) % 4, (x + 3) % 4, (x + 2) % 4
    yp, ym, yo = (y + 1) % 4, (y + 3) % 4, (y + 2) % 4
    zp, zm = (z + 1) % 8, (z + 7) % 8
    yh = y // 2

    own = [
        pltpu.make_async_copy(piv.at[pl.ds(NR * h, NR)], ag.at[:, x, h], l_ss.at[0]),
        pltpu.make_async_copy(pat_h, pat, l_ss.at[1]),
        pltpu.make_async_copy(low, bg.at[y, h], l_ss.at[2]),
        pltpu.make_async_copy(dia_h, am, l_ss.at[3]),
        pltpu.make_async_copy(pan_h, pan, l_ss.at[4]),
    ]
    for c in own:
        c.start()

    def dev(zz, hh, xx, yy):
        return (2 * zz + hh, 4 * xx + yy)

    def rcopy(src, dst, ss, rs, to):
        return pltpu.make_async_remote_copy(
            src_ref=src, dst_ref=dst, send_sem=ss, recv_sem=rs, device_id=to, device_id_type=MESH
        )

    here = dev(z, oh, x, y)

    def arrived(slot, ss, rs):
        rcopy(slot, slot, ss, rs, here).wait_recv()

    peers = [here, dev(zp, h, x, y), dev(zm, h, x, y)]
    for hh in (h, oh):
        peers += [dev(z, hh, xx, y) for xx in (xp, xm, xo)]
        peers += [dev(z, hh, x, yy) for yy in (yp, ym, yo)]
    bar = pltpu.get_barrier_semaphore()
    for p in peers:
        pl.semaphore_signal(bar, inc=1, device_id=p, device_id_type=MESH)
    pl.semaphore_wait(bar, len(peers))

    def rows(hh, i):
        return pl.ds(pl.multiple_of(2 * B * hh + RB * i, RB), RB)

    pending = []

    def go(c):
        c.start()
        pending.append(c)

    def send_a(i):
        for n, hh in enumerate((h, oh)):
            src = piv.at[NR * hh + i]
            go(rcopy(src, ag.at[i, x, h], a_ss.at[i, 2 * n], a_rs.at[i, 1, h], dev(z, hh, xp, y)))
            go(rcopy(src, ag.at[i, x, h], a_ss.at[i, 1 + 2 * n], a_rs.at[i, 2, h], dev(z, hh, xm, y)))

    go(rcopy(piv.at[pl.ds(NR * oh, NR)], ag.at[:, x, h], b_ss.at[9], b_rs.at[9], here))
    go(rcopy(low, bg.at[y, h], b_ss.at[1], b_rs.at[1], dev(z, h, x, yp)))
    go(rcopy(low, bg.at[y, h], b_ss.at[2], b_rs.at[2], dev(z, h, x, ym)))
    send_a(0)
    go(rcopy(low, bg.at[y, h], b_ss.at[0], b_rs.at[0], here))

    def weight(xr, i, kap, kb):
        return pat[4 * (4 * xr + y) + 2 * h + i // 2, 2 * (2 * z + kap) + kb].astype(F32)

    own[0].wait()
    own[1].wait()
    arrived(ag.at[:, x, oh], b_ss.at[9], b_rs.at[9])
    for t in range(2):
        m = jnp.concatenate(
            [
                jnp.concatenate(
                    [
                        ag[i, x, kap, :, kb * B : (kb + 1) * B] * weight(x, i, kap, kb)
                        for kap in range(2)
                        for kb in range(2)
                    ],
                    axis=1,
                )
                for i in (2 * t, 2 * t + 1)
            ],
            axis=0,
        )
        ds[t] = lax.dot_general(
            m, m, (((1,), (1,)), ((), ())), precision=HIGHEST, preferred_element_type=F32
        )

    d0 = (z - 2 * x - yh + 8) % 8

    def takes_down(d, s):
        return (d <= 3) if s == 0 else (d <= 2)

    def takes_up(d, s):
        return (d >= 6) | (d == 0) if s == 0 else (d >= 5) | (d == 0)

    def gives_down(d, s):
        return (d >= 1) & (d <= 4) if s == 0 else (d >= 1) & (d <= 3)

    def gives_up(d, s):
        return (d >= 5) if s == 0 else (d >= 4)

    def dsum_step(t, u, leaf):
        at = pl.ds(RB * u, RB)
        k = 2 * t + u
        tk_d, tk_u = takes_down(d0, t), takes_up(d0, t)
        if not leaf:

            @pl.when(tk_d)
            def _():
                arrived(dsd.at[t, at], d_ss.at[k], dd_rs.at[k])
                ds[t, at, :] += dsd[t, at, :]

            @pl.when(tk_u)
            def _():
                arrived(dsu.at[t, at], d_ss.at[k], du_rs.at[k])
                ds[t, at, :] += dsu[t, at, :]

        first = jnp.logical_not(tk_d | tk_u)
        turn = first if leaf else jnp.logical_not(first)

        @pl.when(turn & gives_down(d0, t))
        def _():
            rcopy(ds.at[t, at], dsd.at[t, at], d_ss.at[k], dd_rs.at[k], dev(zm, h, x, y)).start()

        @pl.when(turn & gives_up(d0, t))
        def _():
            rcopy(ds.at[t, at], dsu.at[t, at], d_ss.at[k], du_rs.at[k], dev(zp, h, x, y)).start()

    def forward_b():
        arrived(bg.at[ym, h], b_ss.at[1], b_rs.at[1])
        go(rcopy(bg.at[ym, h, 0:B], bg.at[ym, h, 0:B], b_ss.at[3], b_rs.at[3], dev(z, h, x, yp)))
        go(rcopy(bg.at[ym, h], bg.at[ym, h], b_ss.at[5], b_rs.at[5], here))
        arrived(bg.at[yp, h], b_ss.at[2], b_rs.at[2])
        go(rcopy(bg.at[yp, h, B:], bg.at[yp, h, B:], b_ss.at[4], b_rs.at[4], dev(z, h, x, ym)))
        go(rcopy(bg.at[yp, h], bg.at[yp, h], b_ss.at[6], b_rs.at[6], here))

    def far_b():
        return (
            rcopy(bg.at[yo, h, 0:B], bg.at[yo, h, 0:B], b_ss.at[7], b_rs.at[7], here),
            rcopy(bg.at[yo, h, B:], bg.at[yo, h, B:], b_ss.at[8], b_rs.at[8], here),
        )

    def forward_b2():
        lower, upper = far_b()
        arrived(bg.at[yo, h, 0:B], b_ss.at[3], b_rs.at[3])
        lower.start()
        arrived(bg.at[yo, h, B:], b_ss.at[4], b_rs.at[4])
        upper.start()

    def build_b():
        own[2].wait()
        arrived(bg.at[y, oh], b_ss.at[0], b_rs.at[0])
        arrived(bg.at[ym, oh], b_ss.at[5], b_rs.at[5])
        arrived(bg.at[yp, oh], b_ss.at[6], b_rs.at[6])
        arrived(bg.at[yo, oh, 0:B], b_ss.at[7], b_rs.at[7])
        arrived(bg.at[yo, oh, B:], b_ss.at[8], b_rs.at[8])
        for yy in range(4):
            for kap in range(2):
                hi, lo = split(bg[yy, kap])
                bh[kap * 256 : kap * 256 + 256, yy * B : yy * B + B] = hi
                bl[kap * 256 : kap * 256 + 256, yy * B : yy * B + B] = lo

    def forward_a(i):
        arrived(ag.at[i, xm, 0], a_ss.at[i, 0], a_rs.at[i, 1, 0])
        go(rcopy(ag.at[i, xm, 0], ag.at[i, xm, 0], af_ss.at[i, 0], a_rs.at[i, 3, 0], dev(z, h, xp, y)))
        arrived(ag.at[i, xp, 1], a_ss.at[i, 0], a_rs.at[i, 2, 1])
        go(rcopy(ag.at[i, xp, 1], ag.at[i, xp, 1], af_ss.at[i, 1], a_rs.at[i, 3, 1], dev(z, h, xm, y)))

    def product(i):
        arrived(ag.at[i, xm, 1], a_ss.at[i, 0], a_rs.at[i, 1, 1])
        arrived(ag.at[i, xp, 0], a_ss.at[i, 0], a_rs.at[i, 2, 0])
        arrived(ag.at[i, xo, 0], a_ss.at[i, 0], a_rs.at[i, 3, 0])
        arrived(ag.at[i, xo, 1], a_ss.at[i, 0], a_rs.at[i, 3, 1])
        for xr in range(4):
            for kap in range(2):
                for kb in range(2):
                    v = ag[i, xr, kap, :, kb * B : (kb + 1) * B] * weight(xr, i, kap, kb)
                    hi, lo = split(v)
                    k = (2 * kap + kb) * B
                    lh[xr * RB : xr * RB + RB, k : k + B] = hi
                    ll[xr * RB : xr * RB + RB, k : k + B] = lo
        p = jnp.dot(lh[...], bh[...], preferred_element_type=F32)
        p += jnp.dot(ll[...], bh[...], preferred_element_type=F32)
        p += jnp.dot(lh[...], bl[...], preferred_element_type=F32)
        for xr in range(4):
            part[i, xr] = p[xr * RB : xr * RB + RB]

    par = (z + yh) % 2
    odd, even = par == 1, par == 0
    e = (z - yh + 8) % 8
    offs = [jnp.where(even, ev, od) for ev, od in ((4, 3), (2, 5), (6, 1), (0, 7))]
    blks = [((e - d + 8) // 2) % 4 for d in offs]

    def reduce_step(i, q, s, leaf):
        d, xr = offs[q], blks[q]
        at = pl.ds(256 * s, 256)
        mine = part.at[i, xr, :, at]
        ss = r_ss.at[i, q, s]
        tk_d, tk_u = takes_down(d, s), takes_up(d, s)
        if not leaf:

            @pl.when(tk_d)
            def _():
                arrived(sd.at[i, xr, s], ss, rd_rs.at[i, xr, s])
                part[i, xr, :, at] += sd[i, xr, s]

            @pl.when(tk_u)
            def _():
                arrived(su.at[i, xr, s], ss, ru_rs.at[i, xr, s])
                part[i, xr, :, at] += su[i, xr, s]

        first = jnp.logical_not(tk_d | tk_u)
        turn = first if leaf else jnp.logical_not(first)

        @pl.when(turn & gives_down(d, s))
        def _():
            rcopy(mine, sd.at[i, xr, s], ss, rd_rs.at[i, xr, s], dev(zm, h, x, y)).start()

        @pl.when(turn & gives_up(d, s))
        def _():
            rcopy(mine, su.at[i, xr, s], ss, ru_rs.at[i, xr, s], dev(zp, h, x, y)).start()

    c_to = y % 2

    def leaves(i):
        for q in range(2):
            for s in range(2):
                reduce_step(i, q, s, True)

    def stage1(i):
        reduce_step(i, 0, 0, False)
        reduce_step(i, 1, 1, False)

    def stage2(i):
        reduce_step(i, 1, 1, False)
        reduce_step(i, 2, 0, False)
        reduce_step(i, 1, 0, False)
        reduce_step(i, 2, 1, False)

    def stage3(i):
        reduce_step(i, 2, 1, False)
        reduce_step(i, 3, 0, False)
        reduce_step(i, 2, 0, False)
        reduce_step(i, 3, 1, False)

    def stage4(i):
        for s in range(2):
            reduce_step(i, 3, s, False)
            for yy in (2 * s, 2 * s + 1):
                same = (yy == y) & (h == c_to)
                src = part.at[i, blks[3], :, pl.ds(B * yy, B)]

                @pl.when(same)
                def _():
                    upd[rows(h, i), :] = part[i, blks[3], :, pl.ds(B * yy, B)]

                @pl.when(jnp.logical_not(same))
                def _():
                    rcopy(
                        src, upd.at[rows(h, i)], y_ss.at[i, yy], y_rs.at[i, h], dev(z, c_to, x, yy)
                    ).start()

    root = d0 == 0
    relay = even & (h == c_to)

    def sum_x():
        @pl.when(root)
        def _():
            for t in range(2):
                for n, xx in enumerate((xp, xm, xo)):
                    rcopy(
                        ds.at[t], sb.at[2 * h + t], s1_ss.at[t, n], s1_rs.at[2 * h + t], dev(z, c_to, xx, y)
                    ).start()

                @pl.when(h != c_to)
                def _():
                    rcopy(ds.at[t], sb.at[2 * h + t], s1_ss.at[t, 3], s1_rs.at[2 * h + t], here).start()

                @pl.when(h == c_to)
                def _():
                    sb[2 * h + t] = ds[t]

    def sum_y():
        @pl.when(relay)
        def _():
            for t in range(4):
                @pl.when(jnp.logical_not(root & (h == t // 2)))
                def _():
                    arrived(sb.at[t], s1_ss.at[0, 0], s1_rs.at[t])

                for n, yy in enumerate((yp, ym, yo)):
                    rcopy(sb.at[t], sb.at[t], s2_ss.at[t, n], s2_rs.at[t], dev(z, h, x, yy)).start()

    def start_factor():
        own[3].wait()

        @pl.when(jnp.logical_not(relay))
        def _():
            for t in range(4):
                arrived(sb.at[t], s2_ss.at[t, 0], s2_rs.at[t])

        am[...] = am[...] - sb[...]
        eye = (
            lax.broadcasted_iota(jnp.int32, (B, B), 0) == lax.broadcasted_iota(jnp.int32, (B, B), 1)
        ).astype(F32)
        for m in range(4):
            mi[m] = eye

    near = (d0 <= 1) | (d0 == 7)
    pieces = [(t, u) for t in range(2) for u in range(2)]
    for t, u in pieces:
        dsum_step(t, u, True)
    forward_a(0)
    send_a(1)
    forward_b()
    pl.when(near)(forward_b2)
    for t, u in pieces:
        dsum_step(t, u, False)
    sum_x()
    pl.when(jnp.logical_not(near))(forward_b2)
    pending.extend(far_b())
    build_b()

    def on_odd(*steps):
        @pl.when(odd)
        def _():
            for f, i in steps:
                f(i)

    def on_even(*steps):
        @pl.when(even)
        def _():
            for f, i in steps:
                f(i)

    for i in range(NR):
        product(i)
        leaves(i)
        if i + 1 < NR:
            forward_a(i + 1)
        if i + 2 < NR:
            send_a(i + 2)
        if i == 2:
            sum_y()
        on_odd(*([(stage1, i)] + ([(stage3, i - 2)] if i >= 2 else [])))
        on_even(*(([(stage2, i - 1)] if i >= 1 else []) + ([(stage4, i - 3)] if i >= 3 else [])))
    start_factor()
    factor_panel(0, am, mi, fac)
    on_odd((stage3, 2))
    on_even((stage2, 3), (stage4, 1))
    factor_panel(1, am, mi, fac)
    on_odd((stage3, 3))
    on_even((stage4, 2))
    factor_panel(2, am, mi, fac)
    on_even((stage4, 3))
    factor_panel(3, am, mi, fac)
    fac_out = pltpu.make_async_copy(fac, fac_h, l_ss.at[5])
    fac_out.start()

    own[4].wait()
    y_src = 2 * (z % 2) + h
    for i in range(NR):
        for hh in range(2):

            @pl.when(jnp.logical_not((y == y_src) & (h == hh)))
            def _():
                arrived(upd.at[rows(hh, i)], y_ss.at[i, 0], y_rs.at[i, hh])

    for m in range(4):
        at = slice(m * B, m * B + B)
        out[at, :] = jnp.dot(
            mi[m], pan[at, :] - upd[at, :], precision=HIGHEST, preferred_element_type=F32
        )
    panel_out = pltpu.make_async_copy(out, out_h, l_ss.at[6])
    panel_out.start()

    for c in pending:
        c.wait_send()
    for t, u in pieces:
        k = 2 * t + u
        at = pl.ds(RB * u, RB)

        @pl.when(jnp.logical_not(root))
        def _():
            rcopy(ds.at[t, at], dsd.at[t, at], d_ss.at[k], dd_rs.at[k], here).wait_send()

    for i in range(NR):
        for q in range(4):
            for s in range(2):

                @pl.when(offs[q] != 0)
                def _():
                    rcopy(
                        part.at[i, blks[q], :, pl.ds(256 * s, 256)], sd.at[i, blks[q], s],
                        r_ss.at[i, q, s], rd_rs.at[i, blks[q], s], here,
                    ).wait_send()

        @pl.when(even)
        def _():
            for yy in range(4):
                @pl.when(jnp.logical_not((yy == y) & (h == c_to)))
                def _():
                    rcopy(
                        part.at[i, blks[3], :, pl.ds(B * yy, B)], upd.at[rows(h, i)],
                        y_ss.at[i, yy], y_rs.at[i, h], here,
                    ).wait_send()

    @pl.when(root)
    def _():
        for t in range(2):
            for n in range(3):
                rcopy(ds.at[t], sb.at[t], s1_ss.at[t, n], s1_rs.at[t], here).wait_send()

            @pl.when(h != c_to)
            def _():
                rcopy(ds.at[t], sb.at[t], s1_ss.at[t, 3], s1_rs.at[t], here).wait_send()

    @pl.when(relay)
    def _():
        for t in range(4):
            for n in range(3):
                rcopy(sb.at[t], sb.at[t], s2_ss.at[t, n], s2_rs.at[t], here).wait_send()

    fac_out.wait()
    panel_out.wait()


def window(pattern, pivot_rows, lower_cols, panel_in, diag_in):
    anyspace = pl.BlockSpec(memory_space=pltpu.HBM)
    dma = pltpu.SemaphoreType.DMA
    return pl.pallas_call(
        window_kernel,
        out_shape=(
            jax.ShapeDtypeStruct((4 * B, B), F32),
            jax.ShapeDtypeStruct((4, B, B), F32),
        ),
        in_specs=[anyspace] * 5,
        out_specs=(anyspace, anyspace),
        scratch_shapes=[
            pltpu.SMEM((64, 32), jnp.int32),
            pltpu.VMEM((NR, 4, 2, RB, 256), F32),
            pltpu.VMEM((4, 2, 256, B), F32),
            pltpu.VMEM((512, 512), BF16),
            pltpu.VMEM((512, 512), BF16),
            pltpu.VMEM((4 * RB, 512), BF16),
            pltpu.VMEM((4 * RB, 512), BF16),
            pltpu.VMEM((NR, 4, RB, 512), F32),
            pltpu.VMEM((NR, 4, 2, RB, 256), F32),
            pltpu.VMEM((NR, 4, 2, RB, 256), F32),
            pltpu.VMEM((4 * B, B), F32),
            pltpu.VMEM((2, B, B), F32),
            pltpu.VMEM((2, B, B), F32),
            pltpu.VMEM((2, B, B), F32),
            pltpu.VMEM((4, B, B), F32),
            pltpu.VMEM((4 * B, B), F32),
            pltpu.VMEM((4, B, B), F32),
            pltpu.VMEM((4, B, B), F32),
            pltpu.VMEM((4, B, B), F32),
            pltpu.VMEM((4 * B, B), F32),
            dma((7,)), dma((NR, 4)), dma((NR, 4, 2)), dma((NR, 2)), dma((10,)), dma((10,)),
            dma((NR, 4, 2)), dma((NR, 4, 2)), dma((NR, 4, 2)), dma((4,)), dma((4,)), dma((4,)),
            dma((2, 4)), dma((4,)), dma((4, 3)), dma((4,)), dma((NR, 4)), dma((NR, 2)),
        ],
        compiler_params=pltpu.CompilerParams(
            collective_id=0, has_side_effects=True, vmem_limit_bytes=60 << 20
        ),
        name="window",
    )(pattern, pivot_rows.reshape(2 * NR, RB, 256), lower_cols, panel_in, diag_in)


def shards(lower_cols, pivot_rows, pattern, panel_in, diag_in):
    return window(pattern, pivot_rows, lower_cols, panel_in, diag_in)


def solution(mesh):
    in_specs = (P("col", "row"), P("row", "col"), P(), P("col", "row"), P("col", None, None))
    out_specs = (P("col", "row"), P("col", None, None))
    return jax.shard_map(shards, mesh=mesh, in_specs=in_specs, out_specs=out_specs, check_vma=False)
```

time: 104 us -> 71.9 us (0.69)
  Pallas kernels: 96.7 us -> 66.3 us
  local copies, waits for them, and re-layouts: 6.03 us -> 3.83 us
    pallas_call x2 -> x1, Pallas kernels: 96.7 us -> 66.3 us  [window(): pl.pallas_call(window_kernel, out_shape=(jax.ShapeDtypeStruct((4 * B, B),...]
    unnamed x13 -> x5, local copies, waits for them, and re-layouts: 6.03 us -> 3.83 us
where the time goes in v2:
time: 71.9 us; the launch traced here: 70.8 us
  Pallas kernels  66.3 us (92%)
  local copies, waits for them, and re-layouts  3.83 us (5%)
    pallas_call x1, Pallas kernels, window(): pl.pallas_call(window_kernel, out_shape=(jax.ShapeDtypeStruct((4 * B, B),...  66.3 us
    unnamed x5, local copies, waits for them, and re-layouts  3.83 us

profile of v2, /device:TPU:22, one launch (start us, length us, event | category | flops | bytes accessed | tf_op | source)
XLA Modules:
  0.0 70.8 jit_solution(14153918177277078128)
XLA Ops:
  0.6 1.4 %copy.7.pat_h = s32[64,32]{1,0:T(8,128)} copy(s32[64,32]{0,1:T(8,128)} %param.7) | data formatting | bytes 16384 | tf_op args[2]
  2.0 66.3 %window.1 = (f32[512,128]{1,0:T(8,128)}, f32[4,128,128]{2,1,0:T(8,128)}) custom-call(s32[64,32]{1,0:T(8,128)} %copy.7.pat_h, f32[8,64,256]{2,1,0:T(8,128)} %bitcast.1, f32[256,128]{1,0:T(8,128)} %low.1, f32[512,128]{1,0:T(8,128)} %pan_h.1, f32[4,128,128]{2,1,0:T(8,128)} %dia_h.1), custom_call_target="tpu_custom_call" | custom-call | tf_op jit(solution)/shard_map/window/pallas_call | solution.py:520
  68.4 0.0 copy-start
  68.4 1.7 %copy.10 = f32[512,128]{1,0:T(8,128)} copy(f32[512,128]{1,0:T(8,128)} %get-tuple-element.4) | data formatting | bytes 524288
  70.1 0.0 copy-done
  70.1 0.7 copy.11
Async XLA Ops:
  68.4 1.7 %copy-start = (f32[4,128,128]{2,1,0:T(8,128)S(1)}, f32[4,128,128]{2,1,0:T(8,128)}, u32[]{:S(2)}) copy-start(f32[4,128,128]{2,1,0:T(8,128)} %get-tuple-element.5) | copy-start | bytes 786436

commit v3 on v2

--- a/solution.py
+++ b/solution.py
@@ -150,7 +150,7 @@
     go(rcopy(low, bg.at[y, h], b_ss.at[0], b_rs.at[0], here))
 
     def weight(xr, i, kap, kb):
-        return pat[4 * (4 * xr + y) + 2 * h + i // 2, 2 * (2 * z + kap) + kb].astype(F32)
+        return pat[2 * (2 * z + kap) + kb, 4 * (4 * xr + y) + 2 * h + i // 2].astype(F32)
 
     own[0].wait()
     own[1].wait()
@@ -223,18 +223,11 @@
         go(rcopy(bg.at[yp, h, B:], bg.at[yp, h, B:], b_ss.at[4], b_rs.at[4], dev(z, h, x, ym)))
         go(rcopy(bg.at[yp, h], bg.at[yp, h], b_ss.at[6], b_rs.at[6], here))
 
-    def far_b():
-        return (
-            rcopy(bg.at[yo, h, 0:B], bg.at[yo, h, 0:B], b_ss.at[7], b_rs.at[7], here),
-            rcopy(bg.at[yo, h, B:], bg.at[yo, h, B:], b_ss.at[8], b_rs.at[8], here),
-        )
-
     def forward_b2():
-        lower, upper = far_b()
         arrived(bg.at[yo, h, 0:B], b_ss.at[3], b_rs.at[3])
-        lower.start()
+        go(rcopy(bg.at[yo, h, 0:B], bg.at[yo, h, 0:B], b_ss.at[7], b_rs.at[7], here))
         arrived(bg.at[yo, h, B:], b_ss.at[4], b_rs.at[4])
-        upper.start()
+        go(rcopy(bg.at[yo, h, B:], bg.at[yo, h, B:], b_ss.at[8], b_rs.at[8], here))
 
     def build_b():
         own[2].wait()
@@ -397,49 +390,58 @@
 
     near = (d0 <= 1) | (d0 == 7)
     pieces = [(t, u) for t in range(2) for u in range(2)]
+
+    def chain():
+        for t, u in pieces:
+            dsum_step(t, u, False)
+
+    def on_odd(*steps):
+        @pl.when(odd)
+        def _():
+            for f, i in steps:
+                f(i)
+
+    def on_even(*steps):
+        @pl.when(even)
+        def _():
+            for f, i in steps:
+                f(i)
+
     for t, u in pieces:
         dsum_step(t, u, True)
+    send_a(1)
     forward_a(0)
-    send_a(1)
     forward_b()
-    pl.when(near)(forward_b2)
-    for t, u in pieces:
-        dsum_step(t, u, False)
-    sum_x()
-    pl.when(jnp.logical_not(near))(forward_b2)
-    pending.extend(far_b())
+    send_a(2)
+    pl.when(jnp.logical_not(near))(chain)
+    forward_b2()
     build_b()
-
-    def on_odd(*steps):
-        @pl.when(odd)
-        def _():
-            for f, i in steps:
-                f(i)
-
-    def on_even(*steps):
-        @pl.when(even)
-        def _():
-            for f, i in steps:
-                f(i)
+    product(0)
+    leaves(0)
+    forward_a(1)
+    send_a(3)
+
+    @pl.when(near)
+    def _():
+        chain()
+        sum_x()
 
     for i in range(NR):
-        product(i)
-        leaves(i)
-        if i + 1 < NR:
-            forward_a(i + 1)
-        if i + 2 < NR:
-            send_a(i + 2)
+        if i > 0:
+            product(i)
+            leaves(i)
+            if i + 1 < NR:
+                forward_a(i + 1)
         if i == 2:
             sum_y()
-        on_odd(*([(stage1, i)] + ([(stage3, i - 2)] if i >= 2 else [])))
-        on_even(*(([(stage2, i - 1)] if i >= 1 else []) + ([(stage4, i - 3)] if i >= 3 else [])))
+        on_odd(*([(stage1, i)] + ([(stage3, i - 1)] if i >= 1 else [])))
+        on_even(*(([(stage2, i - 1)] if i >= 1 else []) + ([(stage4, i - 2)] if i >= 2 else [])))
+    on_even((stage2, 3))
     start_factor()
     factor_panel(0, am, mi, fac)
-    on_odd((stage3, 2))
-    on_even((stage2, 3), (stage4, 1))
-    factor_panel(1, am, mi, fac)
     on_odd((stage3, 3))
     on_even((stage4, 2))
+    factor_panel(1, am, mi, fac)
     factor_panel(2, am, mi, fac)
     on_even((stage4, 3))
     factor_panel(3, am, mi, fac)
@@ -526,7 +528,7 @@
         in_specs=[anyspace] * 5,
         out_specs=(anyspace, anyspace),
         scratch_shapes=[
-            pltpu.SMEM((64, 32), jnp.int32),
+            pltpu.SMEM((32, 64), jnp.int32),
             pltpu.VMEM((NR, 4, 2, RB, 256), F32),
             pltpu.VMEM((4, 2, 256, B), F32),
             pltpu.VMEM((512, 512), BF16),
@@ -554,7 +556,7 @@
             collective_id=0, has_side_effects=True, vmem_limit_bytes=60 << 20
         ),
         name="window",
-    )(pattern, pivot_rows.reshape(2 * NR, RB, 256), lower_cols, panel_in, diag_in)
+    )(pattern.T, pivot_rows.reshape(2 * NR, RB, 256), lower_cols, panel_in, diag_in)
 
 
 def shards(lower_cols, pivot_rows, pattern, panel_in, diag_in):

time: 71.9 us -> 66.7 us (0.928)
  the two profiles are of different devices: /device:TPU:22 before, /device:TPU:27 now
where the time goes in v3:
time: 66.7 us; the launch traced here: 66.6 us
  Pallas kernels  63.6 us (95%)
  local copies, waits for them, and re-layouts  2.42 us (4%)
    pallas_call x1, Pallas kernels, window(): pl.pallas_call(window_kernel, out_shape=(jax.ShapeDtypeStruct((4 * B, B),...  63.6 us
    unnamed x4, local copies, waits for them, and re-layouts  2.42 us

profile of v3, /device:TPU:27, one launch (start us, length us, event | category | flops | bytes accessed | tf_op | source)
XLA Modules:
  0.0 66.6 jit_solution(15640484280655899955)
XLA Ops:
  0.6 63.6 %window.1 = (f32[512,128]{1,0:T(8,128)}, f32[4,128,128]{2,1,0:T(8,128)}) custom-call(s32[32,64]{1,0:T(8,128)} %bitcast.3, f32[8,64,256]{2,1,0:T(8,128)} %bitcast.2, f32[256,128]{1,0:T(8,128)} %low.1, f32[512,128]{1,0:T(8,128)} %pan_h.1, f32[4,128,128]{2,1,0:T(8,128)} %dia_h.1), custom_call_target="tpu_custom_call" | custom-call | tf_op jit(solution)/shard_map/window/pallas_call | solution.py:522
  64.2 0.0 copy-start
  64.2 1.7 %copy.9 = f32[512,128]{1,0:T(8,128)} copy(f32[512,128]{1,0:T(8,128)} %get-tuple-element.4) | data formatting | bytes 524288
  65.9 0.0 copy-done
  65.9 0.7 %copy.10 = f32[4,128,128]{2,1,0:T(8,128)} copy(f32[4,128,128]{2,1,0:T(8,128)S(1)} %copy-done) | data formatting | bytes 524288
Async XLA Ops:
  64.2 1.7 %copy-start = (f32[4,128,128]{2,1,0:T(8,128)S(1)}, f32[4,128,128]{2,1,0:T(8,128)}, u32[]{:S(2)}) copy-start(f32[4,128,128]{2,1,0:T(8,128)} %get-tuple-element.5) | copy-start | bytes 786436
